TPU v7x, 256 devices: a whole 4x4x8 slice. The times are simulated.
256 devices in a mesh: st: 128 (over z, x_lo, y, core), row: 2 (over x_hi).
Axes of the slice: x: 4 (x_hi: 2, x_lo: 2; x = x_hi * 2 + x_lo), y: 4, z: 8, core: 2. Of those that a mesh axis runs over, the one named last changes fastest.
Arguments:
- forcing: bfloat16 [2, 128, 1024, 256], P(None, 'st', 'row'), may hold values from -6 to 6
- inverse_first: bfloat16 [2, 128, 1024, 1024], P(None, 'st', 'row'), may hold values from -0.1875 to 0.1875
- lower_first: bfloat16 [2, 128, 1024, 1024], P(None, 'st', 'row'), may hold values from -0.1875 to 0.1875
- upper_first: bfloat16 [2, 128, 1024, 1024], P(None, 'st', 'row'), may hold values from -0.1875 to 0.1875
- inverse_second: bfloat16 [2, 128, 1024, 1024], P(None, 'st', 'row'), may hold values from -0.1875 to 0.1875
- lower_second: bfloat16 [2, 128, 1024, 1024], P(None, 'st', 'row'), may hold values from -0.1875 to 0.1875
- upper_second: bfloat16 [2, 128, 1024, 1024], P(None, 'st', 'row'), may hold values from -0.1875 to 0.1875
Outputs:
- reduced_forcing: bfloat16 [2, 128, 1024, 256], P(None, 'st', 'row')
All inputs are finite; a program needn't handle non-finite values.
Results may differ from a plain program's by a relative error of at most 0.0059.
Values may be sent and summed in bfloat16 or wider, within the bound.
No kernel may reach another device: no remote copies, remote signals or barrier semaphores. Data moves between devices by JAX's collectives and lax.ppermute only.
A program may use at most 64 MiB of HBM per device.

v0:
```python
import jax
import jax.numpy as jnp
from jax import lax
from jax.sharding import PartitionSpec as P


def from_behind(value, axis, steps):
    count = lax.axis_size(axis)
    pairs = [(source, (source + steps) % count) for source in range(count)]
    return lax.ppermute(value, axis, pairs)


def shifted_earlier(received, stride):
    position = lax.axis_index("st")
    earlier = jnp.concatenate([jnp.zeros_like(received[:1]), received[:-1]], axis=0)
    return jnp.where(position < stride, earlier, received)


def shifted_later(received, stride):
    position = lax.axis_index("st")
    later_rows = jnp.concatenate([received[1:], jnp.zeros_like(received[:1])], axis=0)
    return jnp.where(position >= lax.axis_size("st") - stride, later_rows, received)


def product(blocks, vectors):
    return jnp.einsum("jrk,jkc->jrc", blocks, vectors, preferred_element_type=jnp.float32)


def reduce_level(forcing_now, inverse, lower, upper, stride):
    scaled = product(inverse, lax.all_gather(forcing_now, "row", axis=1, tiled=True)).astype(
        jnp.bfloat16
    )
    gathered = lax.all_gather(scaled, "row", axis=1, tiled=True)
    from_below = shifted_earlier(from_behind(gathered, "st", stride), stride)
    from_above = shifted_later(from_behind(gathered, "st", -stride), stride)
    coupled = product(lower, from_below) + product(upper, from_above)
    return (forcing_now.astype(jnp.float32) - coupled).astype(jnp.bfloat16)


def on_device(
    forcing, inverse_first, lower_first, upper_first, inverse_second, lower_second, upper_second
):

    def squeeze(array):
        return array.reshape((array.shape[0],) + array.shape[2:])

    forcing_first = reduce_level(
        squeeze(forcing), squeeze(inverse_first), squeeze(lower_first), squeeze(upper_first), 1
    )
    reduced = reduce_level(
        forcing_first, squeeze(inverse_second), squeeze(lower_second), squeeze(upper_second), 2
    )
    return reduced.reshape(forcing.shape)


def solution(mesh):
    return jax.shard_map(
        on_device,
        mesh=mesh,
        in_specs=(
            P(None, "st", "row", None),
            P(None, "st", "row", None),
            P(None, "st", "row", None),
            P(None, "st", "row", None),
            P(None, "st", "row", None),
            P(None, "st", "row", None),
            P(None, "st", "row", None),
        ),
        out_specs=P(None, "st", "row", None),
        check_vma=False,
    )
```

profile of v0, /device:TPU:1, one launch (start us, length us, event | category | flops | bytes accessed | tf_op | source)
XLA Modules:
  0.0 201.1 jit_solution(2558496426390451680)
XLA Ops:
  6.5 0.0 copy-start
  6.5 0.0 all-gather.12.cloned.1.call-start
  6.5 0.7 all-gather.12.cloned.1.call-update
  7.3 0.0 copy-start.1
  7.3 0.0 all-gather.6.cloned.1.call-start
  7.3 33.3 %all-gather.12.cloned.1.call-done = bf16[2,1,1024,256]{3,2,0,1:T(8,128)(2,1)} async-done(((bf16[2,1,512,256]{3,2,0,1:T(8,128)(2,1)}), bf16[2,1,1024,256]{3,2,0,1:T(8,128)(2,1)}) %all-gather.12.cloned.1.call-update) | async-done | bytes 1048592 | tf_op jit(solution)/shard_map/all_gather | solution.py:30
  40.6 0.0 copy-done
  40.7 2.7 %fusion.27 = bf16[2,512,256]{2,1,0:T(8,128)(2,1)} fusion(bf16[2,1,512,1024]{3,2,1,0:T(8,128)(2,1)S(1)} %copy-done, bf16[2,1,1024,256]{3,2,0,1:T(8,128)(2,1)} %all-gather.12.cloned.1.call-done), kind=kOutput, calls=%fused_computation.17 | convolution fusion | flops 537133056 | bytes 3670016 | tf_op jit(solution)/shard_map/jrk,jkc->jrc/dot_general | solution.py:26
  43.4 0.0 all-gather.6.cloned.1.call-update
  43.4 0.0 all-gather.8.cloned.1.call-start
  43.5 27.4 %all-gather.6.cloned.1.call-done = bf16[2,1024,256]{2,1,0:T(8,128)(2,1)} async-done(((bf16[2,512,256]{2,1,0:T(8,128)(2,1)}), bf16[2,1024,256]{2,1,0:T(8,128)(2,1)}) %all-gather.6.cloned.1.call-update) | async-done | bytes 1048592 | tf_op jit(solution)/shard_map/all_gather | solution.py:33
  70.9 0.8 collective-permute-start.1
  71.7 1.1 collective-permute-start
  72.8 0.0 copy-done.1
  72.8 0.2 copy.8
  73.1 12.9 %collective-permute-done.1 = bf16[2,1024,256]{2,1,0:T(8,128)(2,1)} collective-permute-done((bf16[2,1024,256]{2,1,0:T(8,128)(2,1)}, bf16[2,1024,256]{2,1,0:T(8,128)(2,1)}, u32[]{:S(2)}, u32[]{:S(2)}) %collective-permute-start.1) | collective-permute-done | bytes 1048608 | tf_op jit(solution)/shard_map/ppermute | solution.py:10
  85.9 1.1 slice.17
  87.0 0.0 collective-permute-done
  87.0 1.1 slice.16
  88.1 0.0 copy-start.4
  88.1 2.9 %fusion.6 = f32[2,256,512]{2,1,0:T(8,128)S(1)} fusion(bf16[2,1,512,1024]{3,2,1,0:T(8,128)(2,1)} %param.10, bf16[2,1024,256]{2,1,0:T(8,128)(2,1)} %collective-permute-done.1, bf16[1,1024,256]{2,1,0:T(8,128)(2,1)S(1)} %slice.17, pred[]{:T(512)S(6)} %ge.6), kind=kOutput, calls=%fused_computation.6 | convolution fusion | flops 537395200 | bytes 4718593 | tf_op jit(solution)/shard_map/jrk,jkc->jrc/dot_general | solution.py:26
  91.1 0.0 copy-done.4
  91.1 3.1 %fusion.33 = bf16[2,512,256]{1,2,0:T(8,128)(2,1)} fusion(f32[2,256,512]{2,1,0:T(8,128)S(1)} %fusion.6, bf16[2,1,512,1024]{3,2,1,0:T(8,128)(2,1)S(1)} %copy-done.4, bf16[2,1024,256]{2,1,0:T(8,128)(2,1)} %collective-permute-done, bf16[1,1024,256]{2,1,0:T(8,128)(2,1)S(1)} %slice.16, pred[]{:T(512)S(6)} %lt.6, bf16[2,1,512,256]{2,3,0,1:T(8,128)(2,1)S(1)} %copy.8), kind=kOutput, calls=%fused_computation.19 | convolution fusion | flops 538443776 | bytes 5767169 | tf_op jit(solution)/shard_map/jrk,jkc->jrc/dot_general | solution.py:26
  94.2 0.0 all-gather.8.cloned.1.call-update
  94.2 0.0 all-gather.10.cloned.1.call-start
  94.3 30.5 %all-gather.8.cloned.1.call-done = bf16[2,1024,256]{1,2,0:T(8,128)(2,1)} async-done(((bf16[2,512,256]{1,2,0:T(8,128)(2,1)}), bf16[2,1024,256]{1,2,0:T(8,128)(2,1)}) %all-gather.8.cloned.1.call-update) | async-done | bytes 1048592 | tf_op jit(solution)/shard_map/all_gather | solution.py:30
  124.7 3.5 %fusion.36 = bf16[2,512,256]{1,2,0:T(8,128)(2,1)} fusion(bf16[2,1024,256]{1,2,0:T(8,128)(2,1)} %all-gather.8.cloned.1.call-done, bf16[2,1,512,1024]{3,2,1,0:T(8,128)(2,1)} %param.11), kind=kOutput, calls=%fused_computation.20 | convolution fusion | flops 537133056 | bytes 3670016 | tf_op jit(solution)/shard_map/jrk,jkc->jrc/dot_general | solution.py:26
  128.2 0.0 all-gather.10.cloned.1.call-update
  128.2 27.5 %all-gather.10.cloned.1.call-done = bf16[2,1024,256]{1,2,0:T(8,128)(2,1)} async-done(((bf16[2,512,256]{1,2,0:T(8,128)(2,1)}), bf16[2,1024,256]{1,2,0:T(8,128)(2,1)}) %all-gather.10.cloned.1.call-update) | async-done | bytes 1048592 | tf_op jit(solution)/shard_map/all_gather | solution.py:33
  155.7 5.2 %collective-permute-start.3 = (bf16[2,1024,256]{1,2,0:T(8,128)(2,1)}, bf16[2,1024,256]{1,2,0:T(8,128)(2,1)}, u32[]{:S(2)}, u32[]{:S(2)}) collective-permute-start(bf16[2,1024,256]{1,2,0:T(8,128)(2,1)} %all-gather.10.cloned.1.call-done), channel_id=1, source_target_pairs={{0,252},{2,254},{4,0},{6,2},{8,4},{10,6},{12,8},{14,10},{16,12},{1... | collective-permute-start | bytes 3145736 | tf_op jit(solution)/shard_map/ppermute | solution.py:10
  161.0 0.0 collective-permute-start.2
  161.0 22.0 %collective-permute-done.3 = bf16[2,1024,256]{1,2,0:T(8,128)(2,1)} collective-permute-done((bf16[2,1024,256]{1,2,0:T(8,128)(2,1)}, bf16[2,1024,256]{1,2,0:T(8,128)(2,1)}, u32[]{:S(2)}, u32[]{:S(2)}) %collective-permute-start.3) | collective-permute-done | bytes 1048608 | tf_op jit(solution)/shard_map/ppermute | solution.py:10
  182.9 1.1 slice.19
  184.0 5.0 %collective-permute-done.2 = bf16[2,1024,256]{1,2,0:T(8,128)(2,1)S(1)} collective-permute-done((bf16[2,1024,256]{1,2,0:T(8,128)(2,1)}, bf16[2,1024,256]{1,2,0:T(8,128)(2,1)S(1)}, u32[]{:S(2)}, u32[]{:S(2)}) %collective-permute-start.2) | collective-permute-done | bytes 1048608 | tf_op jit(solution)/shard_map/ppermute | solution.py:10
  189.0 0.0 copy-start.3
  189.0 0.9 copy-done.3
  190.0 0.0 copy-start.2
  190.0 0.0 copy-start.5
  190.0 2.8 %fusion = f32[2,256,512]{2,1,0:T(8,128)S(1)} fusion(bf16[2,1,512,1024]{3,2,1,0:T(8,128)(2,1)} %param.13, bf16[2,1024,256]{1,2,0:T(8,128)(2,1)} %collective-permute-done.3, bf16[1,1024,256]{1,2,0:T(8,128)(2,1)S(1)} %slice.19, pred[]{:T(512)S(6)} %ge.7), kind=kOutput, calls=%fused_computation | convolution fusion | flops 537395200 | bytes 4718593 | tf_op jit(solution)/shard_map/jrk,jkc->jrc/dot_general | solution.py:26
  192.8 0.0 copy-done.2
  192.8 0.0 copy-done.5
  192.8 0.8 fusion.54
  193.6 1.0 copy.12
  (1 shorter events, 0.0 us)
Async XLA Ops:
  6.5 34.1 %copy-start = (bf16[2,1,512,1024]{3,2,1,0:T(8,128)(2,1)S(1)}, bf16[2,1,512,1024]{3,2,1,0:T(8,128)(2,1)}, u32[]{:S(2)}) copy-start(bf16[2,1,512,1024]{3,2,1,0:T(8,128)(2,1)} %param.8) | copy-start | bytes 6291460
  6.5 34.1 %all-gather.12.cloned.1.call-start = ((), (), s32[]{:S(2)}) async-start(), calls=%async_computation.3 | async-start | bytes 1572864 | tf_op jit(solution)/shard_map/all_gather | solution.py:30
  7.3 65.6 %copy-start.1 = (bf16[2,1,512,256]{3,2,1,0:T(8,128)(2,1)S(1)}, bf16[2,1,512,256]{3,2,1,0:T(8,128)(2,1)}, u32[]{:S(2)}) copy-start(bf16[2,1,512,256]{3,2,1,0:T(8,128)(2,1)} %param.7) | copy-start | bytes 1572868
  7.3 63.6 %all-gather.6.cloned.1.call-start = ((), (), s32[]{:S(2)}) async-start(), calls=%async_computation | async-start | bytes 1572864 | tf_op jit(solution)/shard_map/all_gather | solution.py:33
  43.4 81.3 %all-gather.8.cloned.1.call-start = ((), (), s32[]{:S(2)}) async-start(), calls=%async_computation.1 | async-start | bytes 1572864 | tf_op jit(solution)/shard_map/all_gather | solution.py:30
  70.9 15.0 %collective-permute-start.1 = (bf16[2,1024,256]{2,1,0:T(8,128)(2,1)}, bf16[2,1024,256]{2,1,0:T(8,128)(2,1)}, u32[]{:S(2)}, u32[]{:S(2)}) collective-permute-start(bf16[2,1024,256]{2,1,0:T(8,128)(2,1)} %all-gather.6.cloned.1.call-done), channel_id=1, source_target_pairs={{0,254},{2,0},{4,2},{6,4},{8,6},{10,8},{12,10},{14,12},{16,14},{18... | collective-permute-start | bytes 3145736 | tf_op jit(solution)/shard_map/ppermute | solution.py:10
  71.7 15.3 %collective-permute-start = (bf16[2,1024,256]{2,1,0:T(8,128)(2,1)}, bf16[2,1024,256]{2,1,0:T(8,128)(2,1)}, u32[]{:S(2)}, u32[]{:S(2)}) collective-permute-start(bf16[2,1024,256]{2,1,0:T(8,128)(2,1)} %all-gather.6.cloned.1.call-done), channel_id=1, source_target_pairs={{0,2},{2,4},{4,6},{6,8},{8,10},{10,12},{12,14},{14,16},{16,18},{18... | collective-permute-start | bytes 3145736 | tf_op jit(solution)/shard_map/ppermute | solution.py:10
  88.1 3.0 %copy-start.4 = (bf16[2,1,512,1024]{3,2,1,0:T(8,128)(2,1)S(1)}, bf16[2,1,512,1024]{3,2,1,0:T(8,128)(2,1)}, u32[]{:S(2)}) copy-start(bf16[2,1,512,1024]{3,2,1,0:T(8,128)(2,1)} %param.9) | copy-start | bytes 6291460
  94.2 61.5 %all-gather.10.cloned.1.call-start = ((), (), s32[]{:S(2)}) async-start(), calls=%async_computation.2 | async-start | bytes 1572864 | tf_op jit(solution)/shard_map/all_gather | solution.py:33
  155.7 27.2 %collective-permute-start.3 = (bf16[2,1024,256]{1,2,0:T(8,128)(2,1)}, bf16[2,1024,256]{1,2,0:T(8,128)(2,1)}, u32[]{:S(2)}, u32[]{:S(2)}) collective-permute-start(bf16[2,1024,256]{1,2,0:T(8,128)(2,1)} %all-gather.10.cloned.1.call-done), channel_id=1, source_target_pairs={{0,252},{2,254},{4,0},{6,2},{8,4},{10,6},{12,8},{14,10},{16,12},{1... | collective-permute-start | bytes 3145736 | tf_op jit(solution)/shard_map/ppermute | solution.py:10
  161.0 28.0 %collective-permute-start.2 = (bf16[2,1024,256]{1,2,0:T(8,128)(2,1)}, bf16[2,1024,256]{1,2,0:T(8,128)(2,1)S(1)}, u32[]{:S(2)}, u32[]{:S(2)}) collective-permute-start(bf16[2,1024,256]{1,2,0:T(8,128)(2,1)} %all-gather.10.cloned.1.call-done), channel_id=1, source_target_pairs={{0,4},{2,6},{4,8},{6,10},{8,12},{10,14},{12,16},{14,18},{16,20},{1... | collective-permute-start | bytes 3145736 | tf_op jit(solution)/shard_map/ppermute | solution.py:10
  189.0 1.0 copy-start.3
  190.0 2.8 %copy-start.2 = (bf16[2,512,256]{1,2,0:T(8,128)(2,1)S(1)}, bf16[2,512,256]{1,2,0:T(8,128)(2,1)}, u32[]{:S(2)}) copy-start(bf16[2,512,256]{1,2,0:T(8,128)(2,1)} %fusion.33) | copy-start | bytes 1572868
  190.0 2.8 %copy-start.5 = (bf16[2,1,512,1024]{3,2,1,0:T(8,128)(2,1)S(1)}, bf16[2,1,512,1024]{3,2,1,0:T(8,128)(2,1)}, u32[]{:S(2)}) copy-start(bf16[2,1,512,1024]{3,2,1,0:T(8,128)(2,1)} %param.12) | copy-start | bytes 6291460
Sparse Core Ops, SparseCore 0:
  9.1 31.4 all-gather.11
  43.5 27.3 all-gather.5
  94.4 30.3 all-gather.7
  128.4 27.3 all-gather.9
where the time goes:
time: 201 us
  waiting for transfers between devices  159 us (79%)
  matrix products  15.9 us (8%)
  between operations  13.2 us (7%)
  starting transfers between devices  7.28 us (4%)
  local copies, waits for them, and re-layouts  5.44 us (3%)
    all_gather x2, waiting for transfers between devices, reduce_level(): lax.all_gather(forcing_now, 'row', axis=1, tiled=True)  63.8 us
    all_gather x2, waiting for transfers between devices, reduce_level(): gathered = lax.all_gather(scaled, 'row', axis=1, tiled=True)  54.9 us
    ppermute x4, waiting for transfers between devices, from_behind(): return lax.ppermute(value, axis, pairs)  39.8 us
    dot_general x6, matrix products, product(): jnp.einsum('jrk,jkc->jrc', blocks, vectors, preferred_element_type=jnp.fl...  15.9 us
    ppermute x4, starting transfers between devices, from_behind(): return lax.ppermute(value, axis, pairs)  7.15 us
  transfers between devices with their start and end apart: 8, of which 7 were waited for; matrix products, arithmetic and copies ran while one was open for 1% of the time, Pallas kernels for 0%

commit v1 on v0

--- a/solution.py
+++ b/solution.py
@@ -30,7 +30,9 @@
     scaled = product(inverse, lax.all_gather(forcing_now, "row", axis=1, tiled=True)).astype(
         jnp.bfloat16
     )
-    gathered = lax.all_gather(scaled, "row", axis=1, tiled=True)
+    gathered = jnp.concatenate(
+        lax.all_to_all(jnp.stack([scaled] * lax.axis_size("row")), "row", 0, 0), axis=1
+    )
     from_below = shifted_earlier(from_behind(gathered, "st", stride), stride)
     from_above = shifted_later(from_behind(gathered, "st", -stride), stride)
     coupled = product(lower, from_below) + product(upper, from_above)

time: 201 us -> 181 us (0.900)
  waiting for transfers between devices: 159 us -> 102 us
  blocking collectives: 0 us -> 33.7 us
  local copies, waits for them, and re-layouts: 5.44 us -> 7.9 us
    all_gather x2 -> x0, waiting for transfers between devices: 54.9 us -> none  [reduce_level(): gathered = lax.all_gather(scaled, 'row', axis=1, tiled=True)]
    all_to_all x0 -> x2, blocking collectives: none -> 33.7 us  [reduce_level(): lax.all_to_all(jnp.stack([scaled] * lax.axis_size('row')), 'row', 0, 0)]
    reshape x0 -> x2, local copies, waits for them, and re-layouts: none -> 2.36 us  [reduce_level(): jnp.concatenate(lax.all_to_all(jnp.stack([scaled] * lax.axis_size('row'))...]
  transfers between devices with their start and end apart: 8 -> 6, of which waited for: 7 -> 5; matrix products, arithmetic and copies ran while one was open for 1% -> 1% of each run, Pallas kernels for 0% -> 0%
where the time goes in v1:
time: 181 us
  waiting for transfers between devices  102 us (56%)
  blocking collectives  33.7 us (19%)
  matrix products  15.5 us (9%)
  between operations  13.5 us (7%)
  starting transfers between devices  8.01 us (4%)
  local copies, waits for them, and re-layouts  7.9 us (4%)
    all_gather x2, waiting for transfers between devices, reduce_level(): lax.all_gather(forcing_now, 'row', axis=1, tiled=True)  62.1 us
    ppermute x4, waiting for transfers between devices, from_behind(): return lax.ppermute(value, axis, pairs)  38.9 us
    all_to_all x2, blocking collectives, reduce_level(): lax.all_to_all(jnp.stack([scaled] * lax.axis_size('row')), 'row', 0, 0)  33.7 us
    dot_general x6, matrix products, product(): jnp.einsum('jrk,jkc->jrc', blocks, vectors, preferred_element_type=jnp.fl...  15.5 us
    ppermute x4, starting transfers between devices, from_behind(): return lax.ppermute(value, axis, pairs)  7.97 us
  transfers between devices with their start and end apart: 6, of which 5 were waited for; matrix products, arithmetic and copies ran while one was open for 1% of the time, Pallas kernels for 0%

profile of v1, /device:TPU:1, one launch (start us, length us, event | category | flops | bytes accessed | tf_op | source)
XLA Modules:
  0.0 180.6 jit_solution(16584724243607088121)
XLA Ops:
  6.5 0.0 copy-start
  6.5 0.0 all-gather.6.cloned.1.call-start
  6.5 0.7 all-gather.6.cloned.1.call-update
  7.3 0.0 all-gather.4.cloned.1.call-start
  7.3 33.3 %all-gather.6.cloned.1.call-done = bf16[2,1,1024,256]{3,2,0,1:T(8,128)(2,1)} async-done(((bf16[2,1,512,256]{3,2,0,1:T(8,128)(2,1)}), bf16[2,1,1024,256]{3,2,0,1:T(8,128)(2,1)}) %all-gather.6.cloned.1.call-update) | async-done | bytes 1048592 | tf_op jit(solution)/shard_map/all_gather | solution.py:30
  40.6 0.0 copy-done
  40.7 1.9 %fusion.39 = bf16[1,2,512,256]{3,2,1,0:T(8,128)(2,1)S(1)} fusion(bf16[2,1,512,1024]{3,2,1,0:T(8,128)(2,1)S(1)} %copy-done, bf16[2,1,1024,256]{3,2,0,1:T(8,128)(2,1)} %all-gather.6.cloned.1.call-done), kind=kOutput, calls=%fused_computation.21 | convolution fusion | flops 537133056 | bytes 3670016 | tf_op jit(solution)/shard_map/jrk,jkc->jrc/dot_general | solution.py:26
  42.6 0.1 pad_maximum_fusion
  42.7 0.0 copy-start.3
  42.7 16.9 %all_to_all.10 = bf16[2,2,512,256]{3,2,1,0:T(8,128)(2,1)S(1)} all-to-all(bf16[2,2,512,256]{3,2,1,0:T(8,128)(2,1)S(1)} %pad_maximum_fusion), channel_id=1, replica_groups=mesh['st'=128,'row'=2] {'row'}, dimensions={0} | all-to-all | bytes 2097152 | tf_op jit(solution)/shard_map/all_to_all | solution.py:34
  59.6 1.1 copy.13
  60.7 1.7 collective-permute-start.1
  62.4 1.1 collective-permute-start
  63.5 0.0 copy-done.3
  63.5 0.2 copy.11
  63.7 12.9 %collective-permute-done.1 = bf16[2,1024,256]{2,1,0:T(8,128)(2,1)} collective-permute-done((bf16[2,1024,256]{2,1,0:T(8,128)(2,1)}, bf16[2,1024,256]{2,1,0:T(8,128)(2,1)}, u32[]{:S(2)}, u32[]{:S(2)}) %collective-permute-start.1) | collective-permute-done | bytes 1048608 | tf_op jit(solution)/shard_map/ppermute | solution.py:10
  76.6 1.1 slice.17
  77.6 0.0 collective-permute-done
  77.7 1.1 slice.16
  78.7 0.0 copy-start.4
  78.7 2.9 %fusion.6 = f32[2,256,512]{2,1,0:T(8,128)S(1)} fusion(bf16[2,1,512,1024]{3,2,1,0:T(8,128)(2,1)} %param.10, bf16[2,1024,256]{2,1,0:T(8,128)(2,1)} %collective-permute-done.1, bf16[1,1024,256]{2,1,0:T(8,128)(2,1)S(1)} %slice.17, pred[]{:T(512)S(6)} %ge.6), kind=kOutput, calls=%fused_computation.6 | convolution fusion | flops 537395200 | bytes 4718593 | tf_op jit(solution)/shard_map/jrk,jkc->jrc/dot_general | solution.py:26
  81.7 0.0 copy-done.4
  81.7 3.1 %fusion.33 = bf16[2,512,256]{1,2,0:T(8,128)(2,1)} fusion(f32[2,256,512]{2,1,0:T(8,128)S(1)} %fusion.6, bf16[2,1,512,1024]{3,2,1,0:T(8,128)(2,1)S(1)} %copy-done.4, bf16[2,1024,256]{2,1,0:T(8,128)(2,1)} %collective-permute-done, bf16[1,1024,256]{2,1,0:T(8,128)(2,1)S(1)} %slice.16, pred[]{:T(512)S(6)} %lt.6, bf16[2,1,512,256]{2,3,0,1:T(8,128)(2,1)S(1)} %copy.11), kind=kOutput, calls=%fused_computation.19 | convolution fusion | flops 538443776 | bytes 5767169 | tf_op jit(solution)/shard_map/jrk,jkc->jrc/dot_general | solution.py:26
  84.9 0.0 all-gather.4.cloned.1.call-update
  84.9 28.7 %all-gather.4.cloned.1.call-done = bf16[2,1024,256]{1,2,0:T(8,128)(2,1)} async-done(((bf16[2,512,256]{1,2,0:T(8,128)(2,1)}), bf16[2,1024,256]{1,2,0:T(8,128)(2,1)}) %all-gather.4.cloned.1.call-update) | async-done | bytes 1048592 | tf_op jit(solution)/shard_map/all_gather | solution.py:30
  113.6 2.7 %fusion.36 = bf16[1,2,512,256]{2,3,1,0:T(8,128)(2,1)S(1)} fusion(bf16[2,1024,256]{1,2,0:T(8,128)(2,1)} %all-gather.4.cloned.1.call-done, bf16[2,1,512,1024]{3,2,1,0:T(8,128)(2,1)} %param.11), kind=kOutput, calls=%fused_computation.20 | convolution fusion | flops 537133056 | bytes 3670016 | tf_op jit(solution)/shard_map/jrk,jkc->jrc/dot_general | solution.py:26
  116.3 0.1 pad_maximum_fusion.1
  116.4 16.8 %all_to_all.11 = bf16[2,2,512,256]{2,3,1,0:T(8,128)(2,1)S(1)} all-to-all(bf16[2,2,512,256]{2,3,1,0:T(8,128)(2,1)S(1)} %pad_maximum_fusion.1), channel_id=1, replica_groups=mesh['st'=128,'row'=2] {'row'}, dimensions={0} | all-to-all | bytes 2097152 | tf_op jit(solution)/shard_map/all_to_all | solution.py:34
  133.2 1.3 copy.16
  134.5 5.2 %collective-permute-start.3 = (bf16[2,1024,256]{2,1,0:T(8,128)(2,1)}, bf16[2,1024,256]{2,1,0:T(8,128)(2,1)}, u32[]{:S(2)}, u32[]{:S(2)}) collective-permute-start(bf16[2,1024,256]{2,1,0:T(8,128)(2,1)} %bitcast.77), channel_id=1, source_target_pairs={{0,252},{2,254},{4,0},{6,2},{8,4},{10,6},{12,8},{14,10},{16,12},{1... | collective-permute-start | bytes 3145736 | tf_op jit(solution)/shard_map/ppermute | solution.py:10
  139.7 0.0 collective-permute-start.2
  139.7 21.1 %collective-permute-done.3 = bf16[2,1024,256]{2,1,0:T(8,128)(2,1)} collective-permute-done((bf16[2,1024,256]{2,1,0:T(8,128)(2,1)}, bf16[2,1024,256]{2,1,0:T(8,128)(2,1)}, u32[]{:S(2)}, u32[]{:S(2)}) %collective-permute-start.3) | collective-permute-done | bytes 1048608 | tf_op jit(solution)/shard_map/ppermute | solution.py:10
  160.8 1.1 slice.19
  161.8 5.0 %collective-permute-done.2 = bf16[2,1024,256]{2,1,0:T(8,128)(2,1)S(1)} collective-permute-done((bf16[2,1024,256]{2,1,0:T(8,128)(2,1)}, bf16[2,1024,256]{2,1,0:T(8,128)(2,1)S(1)}, u32[]{:S(2)}, u32[]{:S(2)}) %collective-permute-start.2) | collective-permute-done | bytes 1048608 | tf_op jit(solution)/shard_map/ppermute | solution.py:10
  166.8 0.0 copy-start.1
  166.8 0.0 copy-start.2
  166.9 3.0 %fusion = f32[2,256,512]{2,1,0:T(8,128)S(1)} fusion(bf16[2,1,512,1024]{3,2,1,0:T(8,128)(2,1)} %param.13, bf16[2,1024,256]{2,1,0:T(8,128)(2,1)} %collective-permute-done.3, bf16[1,1024,256]{2,1,0:T(8,128)(2,1)S(1)} %slice.19, pred[]{:T(512)S(6)} %ge.7), kind=kOutput, calls=%fused_computation | convolution fusion | flops 537395200 | bytes 4718593 | tf_op jit(solution)/shard_map/jrk,jkc->jrc/dot_general | solution.py:26
  169.8 0.0 copy-done.1
  169.8 0.0 copy-done.2
  169.8 1.9 %fusion.57 = bf16[2,1,512,256]{2,3,0,1:T(8,128)(2,1)} fusion(f32[2,256,512]{2,1,0:T(8,128)S(1)} %fusion, bf16[2,1,512,1024]{3,2,1,0:T(8,128)(2,1)S(1)} %copy-done.1, bf16[2,1024,256]{2,1,0:T(8,128)(2,1)S(1)} %collective-permute-done.2, bf16[1,1024,256]{2,1,0:T(8,128)(2,1)S(1)} %slice.18, pred[]{:T(512)S(6)} %lt.7, bf16[2,512,256]{1,2,0:T(8,128)(2,1)S(1)} %copy-done.2), kind=kOutput, calls=%fused_computation.36 | convolution fusion | flops 538443776 | bytes 5767169 | tf_op jit(solution)/shard_map/jrk,jkc->jrc/dot_general | solution.py:26
  171.7 2.0 %copy.19 = bf16[2,1,512,256]{3,2,1,0:T(8,128)(2,1)} copy(bf16[2,1,512,256]{2,3,0,1:T(8,128)(2,1)} %fusion.57) | data formatting | bytes 1048576 | tf_op jit(solution)/shard_map/reshape | solution.py:55
  (1 shorter events, 0.0 us)
Async XLA Ops:
  6.5 34.1 %copy-start = (bf16[2,1,512,1024]{3,2,1,0:T(8,128)(2,1)S(1)}, bf16[2,1,512,1024]{3,2,1,0:T(8,128)(2,1)}, u32[]{:S(2)}) copy-start(bf16[2,1,512,1024]{3,2,1,0:T(8,128)(2,1)} %param.8) | copy-start | bytes 6291460
  6.5 34.1 %all-gather.6.cloned.1.call-start = ((), (), s32[]{:S(2)}) async-start(), calls=%async_computation.3 | async-start | bytes 1572864 | tf_op jit(solution)/shard_map/all_gather | solution.py:30
  7.3 106.4 %all-gather.4.cloned.1.call-start = ((), (), s32[]{:S(2)}) async-start(), calls=%async_computation.2 | async-start | bytes 1572864 | tf_op jit(solution)/shard_map/all_gather | solution.py:30
  42.7 20.8 %copy-start.3 = (bf16[2,1,512,256]{3,2,1,0:T(8,128)(2,1)S(1)}, bf16[2,1,512,256]{3,2,1,0:T(8,128)(2,1)}, u32[]{:S(2)}) copy-start(bf16[2,1,512,256]{3,2,1,0:T(8,128)(2,1)} %param.7) | copy-start | bytes 1572868
  60.7 15.9 %collective-permute-start.1 = (bf16[2,1024,256]{2,1,0:T(8,128)(2,1)}, bf16[2,1024,256]{2,1,0:T(8,128)(2,1)}, u32[]{:S(2)}, u32[]{:S(2)}) collective-permute-start(bf16[2,1024,256]{2,1,0:T(8,128)(2,1)} %bitcast.6), channel_id=1, source_target_pairs={{0,254},{2,0},{4,2},{6,4},{8,6},{10,8},{12,10},{14,12},{16,14},{18... | collective-permute-start | bytes 3145736 | tf_op jit(solution)/shard_map/ppermute | solution.py:10
  62.4 15.3 %collective-permute-start = (bf16[2,1024,256]{2,1,0:T(8,128)(2,1)}, bf16[2,1024,256]{2,1,0:T(8,128)(2,1)}, u32[]{:S(2)}, u32[]{:S(2)}) collective-permute-start(bf16[2,1024,256]{2,1,0:T(8,128)(2,1)} %bitcast.6), channel_id=1, source_target_pairs={{0,2},{2,4},{4,6},{6,8},{8,10},{10,12},{12,14},{14,16},{16,18},{18... | collective-permute-start | bytes 3145736 | tf_op jit(solution)/shard_map/ppermute | solution.py:10
  78.7 3.0 %copy-start.4 = (bf16[2,1,512,1024]{3,2,1,0:T(8,128)(2,1)S(1)}, bf16[2,1,512,1024]{3,2,1,0:T(8,128)(2,1)}, u32[]{:S(2)}) copy-start(bf16[2,1,512,1024]{3,2,1,0:T(8,128)(2,1)} %param.9) | copy-start | bytes 6291460
  134.5 26.3 %collective-permute-start.3 = (bf16[2,1024,256]{2,1,0:T(8,128)(2,1)}, bf16[2,1024,256]{2,1,0:T(8,128)(2,1)}, u32[]{:S(2)}, u32[]{:S(2)}) collective-permute-start(bf16[2,1024,256]{2,1,0:T(8,128)(2,1)} %bitcast.77), channel_id=1, source_target_pairs={{0,252},{2,254},{4,0},{6,2},{8,4},{10,6},{12,8},{14,10},{16,12},{1... | collective-permute-start | bytes 3145736 | tf_op jit(solution)/shard_map/ppermute | solution.py:10
  139.7 27.1 %collective-permute-start.2 = (bf16[2,1024,256]{2,1,0:T(8,128)(2,1)}, bf16[2,1024,256]{2,1,0:T(8,128)(2,1)S(1)}, u32[]{:S(2)}, u32[]{:S(2)}) collective-permute-start(bf16[2,1024,256]{2,1,0:T(8,128)(2,1)} %bitcast.78), channel_id=1, source_target_pairs={{0,4},{2,6},{4,8},{6,10},{8,12},{10,14},{12,16},{14,18},{16,20},{1... | collective-permute-start | bytes 3145736 | tf_op jit(solution)/shard_map/ppermute | solution.py:10
  166.8 3.0 %copy-start.1 = (bf16[2,1,512,1024]{3,2,1,0:T(8,128)(2,1)S(1)}, bf16[2,1,512,1024]{3,2,1,0:T(8,128)(2,1)}, u32[]{:S(2)}) copy-start(bf16[2,1,512,1024]{3,2,1,0:T(8,128)(2,1)} %param.12) | copy-start | bytes 6291460
  166.8 3.0 %copy-start.2 = (bf16[2,512,256]{1,2,0:T(8,128)(2,1)S(1)}, bf16[2,512,256]{1,2,0:T(8,128)(2,1)}, u32[]{:S(2)}) copy-start(bf16[2,512,256]{1,2,0:T(8,128)(2,1)} %fusion.33) | copy-start | bytes 1572868
Sparse Core Ops, SparseCore 0:
  9.1 31.4 all-gather.5
  85.0 28.5 all-gather.3
